TPU v7x, 256 devices: a whole 4x4x8 slice. The times are simulated.
256 devices in a mesh: aux: 8 (over x_lo, y), occ: 32 (over x_hi, z, core).
Axes of the slice: x: 4 (x_hi: 2, x_lo: 2; x = x_hi * 2 + x_lo), y: 4, z: 8, core: 2. Of those that a mesh axis runs over, the one named last changes fastest.
Arguments:
- factor: bfloat16 [6144, 32, 1536], P('aux', 'occ'), may hold values from -0.67578125 to 0.67578125
- occ_energy: float32 [1024], replicated, may hold values from -3 to -0.5
- vir_energy: float32 [3072], replicated, may hold values from 0.5 to 4
- occ_pick: int32 [32], replicated, may hold values from 0 to 1023
- vir_pick: int32 [1536], replicated, may hold values from 0 to 3071
Outputs:
- gamma: float32 [6144, 32, 1536], P('aux', 'occ')
All inputs are finite; a program needn't handle non-finite values.
Results may differ from a plain program's by a relative error of at most 0.0024.
Values may be sent and summed in bfloat16 or wider, within the bound.
A program may use at most 192 MiB of HBM per device.

v0:
```python
import jax
import jax.numpy as jnp
from jax import lax
from jax.sharding import PartitionSpec as P


def shifted(block, axis, distance):
    devices = range(lax.axis_size(axis))
    route = [((i - distance) % len(devices), i) for i in devices]
    return lax.ppermute(block, axis, route)


def pair_density(left_block, right_block, pair_level, vir_levels, vir_rows):
    integrals = lax.psum_scatter(
        lax.dot_general(
            right_block, left_block, (((0,), (0,)), ((), ())), preferred_element_type=jnp.float32
        ),
        "aux",
        scatter_dimension=0,
        tiled=True,
    )
    divisor = pair_level - vir_rows[:, None] - vir_levels[None, :]
    amplitudes = (integrals / divisor).astype(jnp.bfloat16)
    return jnp.dot(
        right_block,
        lax.all_gather(amplitudes, "aux", axis=0, tiled=True),
        preferred_element_type=jnp.float32,
    )


def on_device(factor, occ_energy, vir_energy, occ_pick, vir_pick):
    aux_count = lax.axis_size("aux")
    occ_count = lax.axis_size("occ")
    aux_place = lax.axis_index("aux")
    occ_place = lax.axis_index("occ")
    local_occ = factor.shape[1]
    virtuals = factor.shape[2]
    row_count = virtuals // aux_count
    occ_levels = jnp.take(occ_energy, occ_pick)
    vir_levels = jnp.take(vir_energy, vir_pick)
    row_start = aux_place * row_count
    vir_rows = lax.dynamic_slice_in_dim(vir_levels, row_start, row_count)
    near_block = shifted(factor, "occ", 1)
    far_block = shifted(near_block, "occ", 1)
    partners = ((1, near_block), (2, far_block))
    left_block = factor[:, 0, :]
    own_level = lax.dynamic_index_in_dim(occ_levels, occ_place * local_occ + 0, keepdims=False)
    density = jnp.zeros((factor.shape[0], virtuals), jnp.float32)
    for distance, block in partners:
        source_base = (occ_place - distance) % occ_count * local_occ
        right_block = block[:, 0, :]
        other_level = lax.dynamic_index_in_dim(occ_levels, source_base + 0, keepdims=False)
        density = density + pair_density(
            left_block, right_block, own_level + other_level, vir_levels, vir_rows
        )
    results = [density]
    return jnp.stack(results, axis=1)


def solution(mesh):
    placed = (P("aux", "occ", None), P(), P(), P(), P())
    return jax.shard_map(
        on_device, mesh=mesh, in_specs=placed, out_specs=P("aux", "occ", None), check_vma=False
    )
```

profile of v0, /device:TPU:1, one launch (start us, length us, event | category | flops | bytes accessed | tf_op | source)
XLA Modules:
  0.0 427.4 jit_solution(7457580632704250876)
XLA Ops:
  6.5 0.0 copy-start
  6.5 0.0 reduce-scatter.3.cloned.1.call-start
  6.5 3.0 collective-permute-start
  9.6 26.1 %collective-permute-done = bf16[768,1,1536]{2,0,1:T(8,128)(2,1)S(1)} collective-permute-done((bf16[768,1,1536]{2,0,1:T(8,128)(2,1)}, bf16[768,1,1536]{2,0,1:T(8,128)(2,1)S(1)}, u32[]{:S(2)}, u32[]{:S(2)}) %collective-permute-start) | collective-permute-done | bytes 2359328 | tf_op jit(solution)/shard_map/ppermute | solution.py:10
  35.7 0.0 copy-start.4
  35.7 1.4 copy-done.4
  37.1 7.9 %fusion.4 = f32[1536,1536]{1,0:T(8,128)} fusion(bf16[768,1,1536]{2,0,1:T(8,128)(2,1)} %param.5, bf16[768,1,1536]{2,0,1:T(8,128)(2,1)S(1)} %collective-permute-done), kind=kOutput, calls=%fused_computation.7 | convolution fusion | flops 3623878656 | bytes 14155776 | tf_op jit(solution)/shard_map/dot_general | solution.py:15
  45.0 0.0 copy-start.3
  45.0 0.0 reduce-scatter.3.cloned.1.call-update
  45.0 0.0 reduce-scatter.5.cloned.1.call-start
  45.1 2.5 collective-permute-start.1
  47.5 26.1 %collective-permute-done.1 = bf16[768,1,1536]{2,0,1:T(8,128)(2,1)S(1)} collective-permute-done((bf16[768,1,1536]{2,0,1:T(8,128)(2,1)}, bf16[768,1,1536]{2,0,1:T(8,128)(2,1)S(1)}, u32[]{:S(2)}, u32[]{:S(2)}) %collective-permute-start.1) | collective-permute-done | bytes 2359328 | tf_op jit(solution)/shard_map/ppermute | solution.py:10
  73.7 0.0 copy-start.6
  73.7 1.4 copy-done.6
  75.1 0.0 copy-done.3
  75.1 6.3 %fusion.1 = f32[1536,1536]{1,0:T(8,128)} fusion(bf16[768,1,1536]{2,0,1:T(8,128)(2,1)S(1)} %collective-permute-done.1, bf16[768,1,1536]{2,0,1:T(8,128)(2,1)S(1)} %copy-done.3), kind=kOutput, calls=%fused_computation.4 | convolution fusion | flops 3623878656 | bytes 14155776 | tf_op jit(solution)/shard_map/dot_general | solution.py:15
  81.4 0.0 copy-start.7
  81.4 0.0 copy-start.1
  81.4 0.0 copy-start.2
  81.4 0.0 reduce-scatter.5.cloned.1.call-update
  81.4 0.0 all-gather.3.cloned.1.call-start
  81.5 0.5 copy-done.7
  82.0 0.0 copy-done.1
  82.1 0.7 gather_fusion
  82.7 0.7 fusion.9
  86.1 0.0 copy-done.2
  86.1 0.0 copy-done
  86.1 8.4 %gather_fusion.1 = f32[1536]{0:T(1024)S(1)} fusion(f32[3072]{0:T(1024)S(1)} %copy-done, s32[2048]{0:T(1024)S(1)} %pad_clamp_fusion), kind=kCustom, calls=%fused_computation.1 | custom fusion | bytes 18432 | tf_op jit(solution)/shard_map/jit(_take)/gather | solution.py:40
  94.5 0.1 dynamic-slice_subtract_fusion
  94.6 80.0 %reduce-scatter.3.cloned.1.call-done = f32[192,1536]{1,0:T(8,128)} async-done(((f32[1536,1536]{1,0:T(8,128)}), f32[192,1536]{1,0:T(8,128)}) %reduce-scatter.3.cloned.1.call-update) | async-done | bytes 1179664 | tf_op jit(solution)/shard_map/reduce_scatter | solution.py:14
  174.6 100.9 %reduce-scatter.5.cloned.1.call-done = f32[192,1536]{1,0:T(8,128)} async-done(((f32[1536,1536]{1,0:T(8,128)}), f32[192,1536]{1,0:T(8,128)}) %reduce-scatter.5.cloned.1.call-update) | async-done | bytes 1179664 | tf_op jit(solution)/shard_map/reduce_scatter | solution.py:14
  275.5 0.0 copy-start.5
  275.5 3.2 divide_convert_fusion
  278.7 0.0 all-gather.3.cloned.1.call-update
  278.7 0.2 all-gather.5.cloned.1.call-start
  279.0 0.3 all-gather.5.cloned.1.call-update
  279.3 58.4 %all-gather.3.cloned.1.call-done = bf16[1536,1536]{1,0:T(8,128)(2,1)} async-done(((bf16[192,1536]{1,0:T(8,128)(2,1)}), bf16[1536,1536]{1,0:T(8,128)(2,1)}) %all-gather.3.cloned.1.call-update) | async-done | bytes 4718608 | tf_op jit(solution)/shard_map/all_gather | solution.py:26
  337.7 0.0 copy-done.5
  337.7 8.4 %fusion.6 = f32[1536,768]{1,0:T(8,128)} fusion(bf16[1536,1536]{1,0:T(8,128)(2,1)} %all-gather.3.cloned.1.call-done, bf16[768,1,1536]{2,0,1:T(8,128)(2,1)S(1)} %copy-done.5), kind=kOutput, calls=%fused_computation.9 | convolution fusion | flops 3623878656 | bytes 11796480 | tf_op jit(solution)/shard_map/dot_general | solution.py:24
  346.2 52.1 %all-gather.5.cloned.1.call-done = bf16[1536,1536]{1,0:T(8,128)(2,1)} async-done(((bf16[192,1536]{1,0:T(8,128)(2,1)}), bf16[1536,1536]{1,0:T(8,128)(2,1)}) %all-gather.5.cloned.1.call-update) | async-done | bytes 4718608 | tf_op jit(solution)/shard_map/all_gather | solution.py:26
  398.3 10.5 %add_bitcast_fusion = f32[768,1,1536]{0,2,1:T(8,128)} fusion(f32[1536,768]{1,0:T(8,128)} %fusion.6, bf16[1536,1536]{1,0:T(8,128)(2,1)} %all-gather.5.cloned.1.call-done, bf16[768,1,1536]{2,0,1:T(8,128)(2,1)} %copy-done.6), kind=kOutput, calls=%fused_computation.2 | convolution fusion | flops 3625058304 | bytes 16515072 | tf_op jit(solution)/shard_map/dot_general | solution.py:24
  408.8 12.1 %copy.7 = f32[768,1,1536]{2,1,0:T(1,128)} copy(f32[768,1,1536]{0,2,1:T(8,128)} %add_bitcast_fusion) | data formatting | bytes 9437184 | tf_op jit(solution)/shard_map/stack | solution.py:57
  (6 shorter events, 0.0 us)
Async XLA Ops:
  6.5 79.6 %copy-start = (f32[3072]{0:T(1024)S(1)}, f32[3072]{0:T(1024)}, u32[]{:S(2)}) copy-start(f32[3072]{0:T(1024)} %param.7) | copy-start | bytes 36868
  6.5 168.1 %reduce-scatter.3.cloned.1.call-start = ((), (), s32[]{:S(2)}) async-start(), calls=%async_computation.2 | async-start | bytes 10616832 | tf_op jit(solution)/shard_map/reduce_scatter | solution.py:14
  6.5 29.1 %collective-permute-start = (bf16[768,1,1536]{2,0,1:T(8,128)(2,1)}, bf16[768,1,1536]{2,0,1:T(8,128)(2,1)S(1)}, u32[]{:S(2)}, u32[]{:S(2)}) collective-permute-start(bf16[768,1,1536]{2,0,1:T(8,128)(2,1)} %param.5), channel_id=1, source_target_pairs={{31,0},{0,1},{1,2},{2,3},{3,4},{4,5},{5,6},{6,7},{7,8},{8,9},{9,10... | collective-permute-start | bytes 7077896 | tf_op jit(solution)/shard_map/ppermute | solution.py:10
  35.7 1.4 copy-start.4
  45.0 30.0 %copy-start.3 = (bf16[768,1,1536]{2,0,1:T(8,128)(2,1)S(1)}, bf16[768,1,1536]{2,0,1:T(8,128)(2,1)}, u32[]{:S(2)}) copy-start(bf16[768,1,1536]{2,0,1:T(8,128)(2,1)} %param.5) | copy-start | bytes 7077892
  45.0 230.5 %reduce-scatter.5.cloned.1.call-start = ((), (), s32[]{:S(2)}) async-start(), calls=%async_computation.4 | async-start | bytes 10616832 | tf_op jit(solution)/shard_map/reduce_scatter | solution.py:14
  45.1 28.6 %collective-permute-start.1 = (bf16[768,1,1536]{2,0,1:T(8,128)(2,1)}, bf16[768,1,1536]{2,0,1:T(8,128)(2,1)S(1)}, u32[]{:S(2)}, u32[]{:S(2)}) collective-permute-start(bf16[768,1,1536]{2,0,1:T(8,128)(2,1)} %copy-done.4), channel_id=1, source_target_pairs={{31,0},{0,1},{1,2},{2,3},{3,4},{4,5},{5,6},{6,7},{7,8},{8,9},{9,10... | collective-permute-start | bytes 7077896 | tf_op jit(solution)/shard_map/ppermute | solution.py:10
  73.7 1.4 copy-start.6
  81.4 0.7 copy-start.7
  81.4 0.7 copy-start.1
  81.4 4.7 %copy-start.2 = (s32[1536]{0:T(1024)S(1)}, s32[1536]{0:T(1024)}, u32[]{:S(2)}) copy-start(s32[1536]{0:T(1024)} %param.9) | copy-start | bytes 18436
  81.4 256.3 %all-gather.3.cloned.1.call-start = ((), (), s32[]{:S(2)}) async-start(), calls=%async_computation.3 | async-start | bytes 5308416 | tf_op jit(solution)/shard_map/all_gather | solution.py:26
  275.5 62.2 %copy-start.5 = (bf16[768,1,1536]{2,0,1:T(8,128)(2,1)S(1)}, bf16[768,1,1536]{2,0,1:T(8,128)(2,1)}, u32[]{:S(2)}) copy-start(bf16[768,1,1536]{2,0,1:T(8,128)(2,1)} %copy-done.4) | copy-start | bytes 7077892
  278.7 119.5 %all-gather.5.cloned.1.call-start = ((), (), s32[]{:S(2)}) async-start(), calls=%async_computation.5 | async-start | bytes 5308416 | tf_op jit(solution)/shard_map/all_gather | solution.py:26
Sparse Core Ops, SparseCore 0:
  45.2 129.3 reduce-scatter.2
  177.1 98.3 reduce-scatter.4
  278.9 58.8 all-gather.2
  339.4 58.8 all-gather.4
where the time goes:
time: 428 us; the launch traced here: 427 us
  waiting for transfers between devices  344 us (80%)
  matrix products  33.2 us (8%)
  local copies, waits for them, and re-layouts  25.2 us (6%)
  between operations  15.9 us (4%)
  starting transfers between devices  5.79 us (1%)
    reduce_scatter x2, waiting for transfers between devices, pair_density(): lax.psum_scatter(lax.dot_general(right_block, left_block, (((0,), (0,)),...  181 us
    all_gather x2, waiting for transfers between devices, pair_density(): lax.all_gather(amplitudes, 'aux', axis=0, tiled=True)  110 us
    ppermute x2, waiting for transfers between devices, shifted(): return lax.ppermute(block, axis, route)  52.2 us
    dot_general x2, matrix products, pair_density(): jnp.dot(right_block, lax.all_gather(amplitudes, 'aux', axis=0, tiled=True...  18.9 us
    dot_general x2, matrix products, pair_density(): lax.dot_general(right_block, left_block, (((0,), (0,)), ((), ())), prefer...  14.2 us
    another operation x1, local copies, waits for them, and re-layouts, on_device(): return jnp.stack(results, axis=1)  12.1 us
  transfers between devices with their start and end apart: 6, of which 6 were waited for; matrix products, arithmetic and copies ran while one was open for 6% of the time, Pallas kernels for 0%

commit v1 on v0

--- a/solution.py
+++ b/solution.py
@@ -23,7 +23,9 @@
     amplitudes = (integrals / divisor).astype(jnp.bfloat16)
     return jnp.dot(
         right_block,
-        lax.all_gather(amplitudes, "aux", axis=0, tiled=True),
+        jnp.concatenate(
+            lax.all_to_all(jnp.stack([amplitudes] * lax.axis_size("aux")), "aux", 0, 0), axis=0
+        ),
         preferred_element_type=jnp.float32,
     )
 

time: 428 us -> 427 us (level)
  waiting for transfers between devices: 344 us -> 279 us
  blocking collectives: 0 us -> 57 us
  starting transfers between devices: 5.79 us -> 10.4 us
    all_gather x2 -> x0, waiting for transfers between devices: 110 us -> none  [pair_density(): lax.all_gather(amplitudes, 'aux', axis=0, tiled=True)]
    all_to_all x0 -> x1, blocking collectives: none -> 57 us  [pair_density(): lax.all_to_all(jnp.stack([amplitudes] * lax.axis_size('aux')), 'aux', 0, 0)]
    all_to_all x0 -> x1, waiting for transfers between devices: none -> 45.6 us  [pair_density(): lax.all_to_all(jnp.stack([amplitudes] * lax.axis_size('aux')), 'aux', 0, 0)]
    all_to_all x0 -> x1, starting transfers between devices: none -> 4.91 us  [pair_density(): lax.all_to_all(jnp.stack([amplitudes] * lax.axis_size('aux')), 'aux', 0, 0)]
  transfers between devices with their start and end apart: 6 -> 5, of which waited for: 6 -> 5; matrix products, arithmetic and copies ran while one was open for 6% -> 6% of each run, Pallas kernels for 0% -> 0%
where the time goes in v1:
time: 427 us; the launch traced here: 426 us
  waiting for transfers between devices  279 us (65%)
  blocking collectives  57 us (13%)
  matrix products  33.5 us (8%)
  local copies, waits for them, and re-layouts  28.2 us (7%)
  between operations  16 us (4%)
  starting transfers between devices  10.4 us (2%)
    reduce_scatter x2, waiting for transfers between devices, pair_density(): lax.psum_scatter(lax.dot_general(right_block, left_block, (((0,), (0,)),...  181 us
    all_to_all x1, blocking collectives, pair_density(): lax.all_to_all(jnp.stack([amplitudes] * lax.axis_size('aux')), 'aux', 0, 0)  57 us
    ppermute x2, waiting for transfers between devices, shifted(): return lax.ppermute(block, axis, route)  52.2 us
    all_to_all x1, waiting for transfers between devices, pair_density(): lax.all_to_all(jnp.stack([amplitudes] * lax.axis_size('aux')), 'aux', 0, 0)  45.6 us
    dot_general x2, matrix products, pair_density(): jnp.dot(right_block, jnp.concatenate(lax.all_to_all(jnp.stack([amplitudes...  18.9 us
    dot_general x2, matrix products, pair_density(): lax.dot_general(right_block, left_block, (((0,), (0,)), ((), ())), prefer...  14.5 us
    another operation x1, local copies, waits for them, and re-layouts, on_device(): return jnp.stack(results, axis=1)  12.1 us
  transfers between devices with their start and end apart: 5, of which 5 were waited for; matrix products, arithmetic and copies ran while one was open for 6% of the time, Pallas kernels for 0%

profile of v1, /device:TPU:1, one launch (start us, length us, event | category | flops | bytes accessed | tf_op | source)
XLA Modules:
  0.0 426.0 jit_solution(16285125298545256216)
XLA Ops:
  6.5 0.0 copy-start
  6.5 0.0 reduce-scatter.3.cloned.1.call-start
  6.5 3.0 collective-permute-start
  9.6 26.1 %collective-permute-done = bf16[768,1,1536]{2,0,1:T(8,128)(2,1)S(1)} collective-permute-done((bf16[768,1,1536]{2,0,1:T(8,128)(2,1)}, bf16[768,1,1536]{2,0,1:T(8,128)(2,1)S(1)}, u32[]{:S(2)}, u32[]{:S(2)}) %collective-permute-start) | collective-permute-done | bytes 2359328 | tf_op jit(solution)/shard_map/ppermute | solution.py:10
  35.7 0.0 copy-start.4
  35.7 1.4 copy-done.4
  37.1 7.9 %fusion.4 = f32[1536,1536]{1,0:T(8,128)} fusion(bf16[768,1,1536]{2,0,1:T(8,128)(2,1)} %param.5, bf16[768,1,1536]{2,0,1:T(8,128)(2,1)S(1)} %collective-permute-done), kind=kOutput, calls=%fused_computation.7 | convolution fusion | flops 3623878656 | bytes 14155776 | tf_op jit(solution)/shard_map/dot_general | solution.py:15
  45.0 0.0 copy-start.3
  45.0 0.0 reduce-scatter.3.cloned.1.call-update
  45.0 0.0 reduce-scatter.5.cloned.1.call-start
  45.1 2.5 collective-permute-start.1
  47.5 26.1 %collective-permute-done.1 = bf16[768,1,1536]{2,0,1:T(8,128)(2,1)S(1)} collective-permute-done((bf16[768,1,1536]{2,0,1:T(8,128)(2,1)}, bf16[768,1,1536]{2,0,1:T(8,128)(2,1)S(1)}, u32[]{:S(2)}, u32[]{:S(2)}) %collective-permute-start.1) | collective-permute-done | bytes 2359328 | tf_op jit(solution)/shard_map/ppermute | solution.py:10
  73.7 0.0 copy-start.6
  73.7 1.4 copy-done.6
  75.0 0.0 copy-done.3
  75.0 6.6 %fusion.1 = f32[1536,1536]{1,0:T(8,128)} fusion(bf16[768,1,1536]{2,0,1:T(8,128)(2,1)S(1)} %collective-permute-done.1, bf16[768,1,1536]{2,0,1:T(8,128)(2,1)S(1)} %copy-done.3), kind=kOutput, calls=%fused_computation.4 | convolution fusion | flops 3623878656 | bytes 14155776 | tf_op jit(solution)/shard_map/dot_general | solution.py:15
  81.6 0.0 copy-start.7
  81.6 0.0 copy-start.1
  81.6 0.0 copy-start.2
  81.6 0.0 reduce-scatter.5.cloned.1.call-update
  81.7 0.6 copy-done.7
  82.3 0.0 copy-done.1
  82.3 0.7 gather_fusion
  83.0 0.6 fusion.9
  86.1 0.0 copy-done.2
  86.1 0.0 copy-done
  86.1 8.4 %gather_fusion.1 = f32[1536]{0:T(1024)S(1)} fusion(f32[3072]{0:T(1024)S(1)} %copy-done, s32[2048]{0:T(1024)S(1)} %pad_clamp_fusion), kind=kCustom, calls=%fused_computation.1 | custom fusion | bytes 18432 | tf_op jit(solution)/shard_map/jit(_take)/gather | solution.py:42
  94.6 0.1 dynamic-slice_subtract_fusion
  94.6 80.0 %reduce-scatter.3.cloned.1.call-done = f32[192,1536]{1,0:T(8,128)} async-done(((f32[1536,1536]{1,0:T(8,128)}), f32[192,1536]{1,0:T(8,128)}) %reduce-scatter.3.cloned.1.call-update) | async-done | bytes 1179664 | tf_op jit(solution)/shard_map/reduce_scatter | solution.py:14
  174.6 100.9 %reduce-scatter.5.cloned.1.call-done = f32[192,1536]{1,0:T(8,128)} async-done(((f32[1536,1536]{1,0:T(8,128)}), f32[192,1536]{1,0:T(8,128)}) %reduce-scatter.5.cloned.1.call-update) | async-done | bytes 1179664 | tf_op jit(solution)/shard_map/reduce_scatter | solution.py:14
  275.5 2.0 divide_convert_fusion
  277.5 0.4 stack.6
  278.0 57.0 %all_to_all.10 = bf16[8,192,1536]{2,1,0:T(8,128)(2,1)} all-to-all(bf16[8,192,1536]{2,1,0:T(8,128)(2,1)S(1)} %stack.6), channel_id=1, replica_groups=mesh['aux'=8,'occ'=32] {'aux'}, dimensions={0} | all-to-all | bytes 9437184 | tf_op jit(solution)/shard_map/all_to_all | solution.py:27
  335.0 2.6 stack.7
  337.6 0.0 copy-start.5
  337.6 4.9 %all-to-all-start.1 = ((bf16[8,192,1536]{2,1,0:T(8,128)(2,1)}), bf16[8,192,1536]{2,1,0:T(8,128)(2,1)}, u32[]{:S(2)}, u32[]{:S(2)}) async-start(bf16[8,192,1536]{2,1,0:T(8,128)(2,1)} %stack.7), calls=%async_computation.3 | async-start | bytes 9437184 | tf_op jit(solution)/shard_map/all_to_all | solution.py:27
  342.5 0.0 copy-done.5
  342.5 8.4 %fusion.6 = f32[1536,768]{1,0:T(8,128)} fusion(bf16[1536,1536]{1,0:T(8,128)(2,1)} %bitcast.25, bf16[768,1,1536]{2,0,1:T(8,128)(2,1)S(1)} %copy-done.5), kind=kOutput, calls=%fused_computation.9 | convolution fusion | flops 3623878656 | bytes 11796480 | tf_op jit(solution)/shard_map/dot_general | solution.py:24
  351.0 45.6 %all-to-all-done.1 = bf16[8,192,1536]{2,1,0:T(8,128)(2,1)} async-done(((bf16[8,192,1536]{2,1,0:T(8,128)(2,1)}), bf16[8,192,1536]{2,1,0:T(8,128)(2,1)}, u32[]{:S(2)}, u32[]{:S(2)}) %all-to-all-start.1) | async-done | bytes 4718624 | tf_op jit(solution)/shard_map/all_to_all | solution.py:27
  396.6 10.5 %add_bitcast_fusion = f32[768,1,1536]{0,2,1:T(8,128)} fusion(f32[1536,768]{1,0:T(8,128)} %fusion.6, bf16[1536,1536]{1,0:T(8,128)(2,1)} %bitcast.6, bf16[768,1,1536]{2,0,1:T(8,128)(2,1)} %copy-done.6), kind=kOutput, calls=%fused_computation.2 | convolution fusion | flops 3625058304 | bytes 16515072 | tf_op jit(solution)/shard_map/dot_general | solution.py:24
  407.1 12.1 %copy.7 = f32[768,1,1536]{2,1,0:T(1,128)} copy(f32[768,1,1536]{0,2,1:T(8,128)} %add_bitcast_fusion) | data formatting | bytes 9437184 | tf_op jit(solution)/shard_map/stack | solution.py:59
  (6 shorter events, 0.0 us)
Async XLA Ops:
  6.5 79.6 %copy-start = (f32[3072]{0:T(1024)S(1)}, f32[3072]{0:T(1024)}, u32[]{:S(2)}) copy-start(f32[3072]{0:T(1024)} %param.7) | copy-start | bytes 36868
  6.5 168.1 %reduce-scatter.3.cloned.1.call-start = ((), (), s32[]{:S(2)}) async-start(), calls=%async_computation.4 | async-start | bytes 10616832 | tf_op jit(solution)/shard_map/reduce_scatter | solution.py:14
  6.5 29.1 %collective-permute-start = (bf16[768,1,1536]{2,0,1:T(8,128)(2,1)}, bf16[768,1,1536]{2,0,1:T(8,128)(2,1)S(1)}, u32[]{:S(2)}, u32[]{:S(2)}) collective-permute-start(bf16[768,1,1536]{2,0,1:T(8,128)(2,1)} %param.5), channel_id=1, source_target_pairs={{31,0},{0,1},{1,2},{2,3},{3,4},{4,5},{5,6},{6,7},{7,8},{8,9},{9,10... | collective-permute-start | bytes 7077896 | tf_op jit(solution)/shard_map/ppermute | solution.py:10
  35.7 1.4 copy-start.4
  45.0 30.0 %copy-start.3 = (bf16[768,1,1536]{2,0,1:T(8,128)(2,1)S(1)}, bf16[768,1,1536]{2,0,1:T(8,128)(2,1)}, u32[]{:S(2)}) copy-start(bf16[768,1,1536]{2,0,1:T(8,128)(2,1)} %param.5) | copy-start | bytes 7077892
  45.0 230.5 %reduce-scatter.5.cloned.1.call-start = ((), (), s32[]{:S(2)}) async-start(), calls=%async_computation.5 | async-start | bytes 10616832 | tf_op jit(solution)/shard_map/reduce_scatter | solution.py:14
  45.1 28.6 %collective-permute-start.1 = (bf16[768,1,1536]{2,0,1:T(8,128)(2,1)}, bf16[768,1,1536]{2,0,1:T(8,128)(2,1)S(1)}, u32[]{:S(2)}, u32[]{:S(2)}) collective-permute-start(bf16[768,1,1536]{2,0,1:T(8,128)(2,1)} %copy-done.4), channel_id=1, source_target_pairs={{31,0},{0,1},{1,2},{2,3},{3,4},{4,5},{5,6},{6,7},{7,8},{8,9},{9,10... | collective-permute-start | bytes 7077896 | tf_op jit(solution)/shard_map/ppermute | solution.py:10
  73.7 1.4 copy-start.6
  81.6 0.7 copy-start.7
  81.6 0.7 copy-start.1
  81.6 4.5 %copy-start.2 = (s32[1536]{0:T(1024)S(1)}, s32[1536]{0:T(1024)}, u32[]{:S(2)}) copy-start(s32[1536]{0:T(1024)} %param.9) | copy-start | bytes 18436
  337.6 4.9 %copy-start.5 = (bf16[768,1,1536]{2,0,1:T(8,128)(2,1)S(1)}, bf16[768,1,1536]{2,0,1:T(8,128)(2,1)}, u32[]{:S(2)}) copy-start(bf16[768,1,1536]{2,0,1:T(8,128)(2,1)} %copy-done.4) | copy-start | bytes 7077892
  337.6 59.0 %all-to-all-start.1 = ((bf16[8,192,1536]{2,1,0:T(8,128)(2,1)}), bf16[8,192,1536]{2,1,0:T(8,128)(2,1)}, u32[]{:S(2)}, u32[]{:S(2)}) async-start(bf16[8,192,1536]{2,1,0:T(8,128)(2,1)} %stack.7), calls=%async_computation.3 | async-start | bytes 9437184 | tf_op jit(solution)/shard_map/all_to_all | solution.py:27
Sparse Core Ops, SparseCore 0:
  45.2 129.3 reduce-scatter.2
  177.2 98.3 reduce-scatter.4
